TPU v7x, 256 devices: a whole 4x4x8 slice. The times are simulated.
256 devices in a mesh: freq: 32 (over y, z), pencil: 8 (over x, core).
Axes of the slice: x: 4, y: 4, z: 8, core: 2. Of those that a mesh axis runs over, the one named last changes fastest.
Arguments:
- wave_field: float32 [64, 512, 2, 512], P('freq', 'pencil'), may hold values from -6 to 6
- source_field: float32 [1, 64, 512, 2, 512], P(None, 'freq', 'pencil'), may hold values from -6 to 6
- omegas: float32 [64], P('freq'), may hold values from 30 to 250
- velocities: float32 [1, 6], replicated, may hold values from 1500 to 4500
- lower_ref: int32 [1, 8, 8], replicated, may hold values from 0 to 4, as said below
- blend_weight: float32 [1, 8, 8], replicated, may hold values from 0 to 1
Outputs:
- new_field: float32 [64, 512, 2, 512], P('freq', 'pencil')
- image: float32 [1, 512, 512], P(None, 'pencil', 'freq')
Inputs may be any that keep to these rules, and one draw needn't show every extreme that they name: `lower_ref`: in each depth step the lower references of one tile row differ by at most one, so a tile row's tiles use at most three consecutive references; in each depth step one tile row uses references 0 to 2 and another references 6 - 3 to 5.
All inputs are finite; a program needn't handle non-finite values.
Results may differ from a plain program's by a relative error of at most 0.0001.
Values sent between devices are 32-bit elements; how exact they have to be, the bound alone decides.
No kernel may reach another device: no remote copies, remote signals or barrier semaphores. Data moves between devices by JAX's collectives and lax.ppermute only.
A program may use at most 128 MiB of HBM per device.

v0:
```python
import functools
import math

import jax
import jax.numpy as jnp
import numpy as np
from jax import lax
from jax.experimental import pallas as pl
from jax.experimental.pallas import tpu as pltpu
from jax.sharding import PartitionSpec as P


N = 512
NREF = 6
NEED = 3
STEP = 10.0
UNIT = 2.0 * math.pi / (N * 12.5)
HALF = N // 2
QUART = N // 4
BF = jnp.bfloat16
F32 = jnp.float32
INTERPRET = False
FIRST = 16


def split(values):
    high = values.astype(BF)
    return high, (values - high.astype(F32)).astype(BF)


def tables():
    place = np.arange(HALF)
    cas = lambda k: (lambda t: np.cos(t) + np.sin(t))((place[:, None] * k[None, :] % N) * (2.0 * np.pi / N)) / np.sqrt(N)
    j = np.arange(QUART)
    fold_even = cas(np.concatenate([2 * j, [HALF], N - 2 * j[1:]]))
    fold_odd = cas(np.concatenate([2 * j + 1, N - 1 - 2 * j]))
    out = []
    for stack in ((fold_even, fold_odd), (fold_even.T, fold_odd.T)):
        table = np.stack(stack)
        high = np.asarray(table, np.float32).astype(jnp.bfloat16)
        low = (table - high.astype(np.float64)).astype(np.float32).astype(jnp.bfloat16)
        out.append(np.stack([high, low], axis=1))
    return out


def dot3(left, right):
    high = jnp.dot(jnp.concatenate(left, axis=0), right[0], preferred_element_type=F32)
    low = jnp.dot(left[0], right[1], preferred_element_type=F32)
    count = left[0].shape[0]
    return high[:count] + (high[count:] + low)


def low_lanes(shape):
    return lax.broadcasted_iota(jnp.int32, shape, len(shape) - 1) < 64


def forward_y(pos_ref, wave_hbm, table_hbm, own0, own1, other0, other1, wave_ref, table_ref, sem):
    pairs = ((wave_hbm, wave_ref), (table_hbm, table_ref))
    copies = [pltpu.make_async_copy(src, dst, sem.at[i]) for i, (src, dst) in enumerate(pairs)]
    for copy in copies:
        copy.start()
    for copy in copies:
        copy.wait()
    rows = jnp.concatenate([wave_ref[f, :, c, :] for f in range(2) for c in range(2)], axis=0)
    near, far = rows[:, :HALF], rows[:, HALF:]
    core = pos_ref[0] % 2
    for kind, outs in ((core, (own0, own1)), (1 - core, (other0, other1))):
        mixed = near + far * (1 - 2 * kind).astype(F32)
        spectrum = dot3(split(mixed), (table_ref[kind, 0], table_ref[kind, 1]))
        for f in range(2):
            for c in range(2):
                start = 128 * f + 64 * c
                outs[f][:, HALF * c : HALF * c + HALF] = spectrum[start : start + 64]


def series(function, degree):
    top = (STEP * 250.0 / 1500.0) ** 2 * 1.0001
    fit = np.polynomial.chebyshev.Chebyshev.interpolate(function, degree, domain=[0.0, top])
    return [float(c) for c in fit.convert(kind=np.polynomial.Polynomial).coef]


COSINE = series(lambda u: np.cos(np.sqrt(u)), 5)
SINE = series(lambda u: np.sinc(np.sqrt(u) / np.pi), 5)


def phase_of(v):
    root = jnp.sqrt(jnp.abs(v))
    u = jnp.maximum(v, 0.0)
    cosine = COSINE[-1] * u + COSINE[-2]
    for c in COSINE[-3::-1]:
        cosine = cosine * u + c
    sine = SINE[-1] * u + SINE[-2]
    for c in SINE[-3::-1]:
        sine = sine * u + c
    moving = v > 0.0
    return jnp.where(moving, cosine, jnp.exp(-root)), jnp.where(moving, sine * root, 0.0)


def rows_of(pos, i):
    return pos + i * (1 - 2 * (pos % 2))


def phases(f, pos_ref, lower_ref, omega_ref, speed_ref, cos_ref, sin_ref, nyq_ref, edge, radial):
    lane = lax.broadcasted_iota(jnp.int32, (QUART, 128), 1)
    row = lax.broadcasted_iota(jnp.int32, (QUART, 128), 0)
    pos = pos_ref[0]
    core = pos % 2
    number = lambda values: values.astype(F32) * (UNIT * STEP)
    ky = number(2 * lane + core)
    ky2 = ky * ky
    bases = [base_of(lower_ref, rows_of(pos, i)) for i in range(2)]
    fix = lane == 128 * core

    def square(t):
        ratio = omega_ref[f] / speed_ref[jnp.where(t < NEED, bases[0] + t, bases[1] + t - NEED)]
        return ratio * ratio * (STEP * STEP)

    squares = jnp.zeros((QUART, 128), F32)
    for t in range(2 * NEED):
        squares = jnp.where(lane // 2 == t, square(t), squares)
    kx = number(2 * row + lane % 2)
    edge[0], edge[1] = phase_of(squares - (kx * kx + (HALF * UNIT * STEP) ** 2))

    for kind in range(2):
        kx = number(2 * row + kind)
        radial[kind] = kx * kx + ky2

    def one(t, carry):
        now = square(t)
        for kind in range(2):
            turn = (128 - 2 * t - kind) % 128
            for k, (ref, part) in enumerate(zip((cos_ref, sin_ref), phase_of(now - radial[kind]))):
                ref[t, kind, :, :128] = part
                ref[t, kind, :, 128:] = jnp.where(fix, pltpu.roll(edge[k], turn, 1), part)
        for half in range(2):
            line = jnp.where(fix[:8], (HALF * UNIT * STEP) ** 2, ky2[:8]) if half else ky2[:8]
            for k, part in enumerate(phase_of(now - ((HALF * UNIT * STEP) ** 2 + line))):
                nyq_ref[t, k, :, 128 * half : 128 * half + 128] = part
        return carry

    lax.fori_loop(0, 2 * NEED, one, 0, unroll=2)


def shift_x(f, pos_ref, *refs):
    cos_ref, sin_ref, nyq_ref, a_ref, b_ref, own_ref, other_ref, wave, spec = refs[-9:]
    if f == 0:
        here, right, left = ((ref.at[0], ref.at[1]) for ref in refs[:3])
    else:
        here, right, left = refs[0:2], refs[2:4], refs[4:6]
    across = refs[-11:-9]
    pos = pos_ref[0]
    chip, core = pos // 2, pos % 2
    sign = lambda flag: jnp.where(flag, 1.0, -1.0).astype(F32)
    mine = sign(chip < 2)
    theirs = sign((chip == 1) | (chip == 2))
    for i in range(2):
        half = 64 * ((core + i) % 2)
        rows = pl.ds(pl.multiple_of(128 * (chip % 2) + half, 64), 64)
        a, b = here[i][...], across[i][...]
        wave[0, rows, :] = a + b
        wave[1, rows, :] = (a - b) * mine
        rows = pl.ds(pl.multiple_of(128 * ((chip + 1) % 2) + half, 64), 64)
        a, b = right[i][...], left[i][...]
        wave[0, rows, :] = a + b
        wave[1, rows, :] = (a - b) * theirs
    for kind in range(2):
        spec[kind] = dot3((a_ref[kind, 0], a_ref[kind, 1]), split(wave[kind]))
    top = lax.broadcasted_iota(jnp.int32, (8, HALF), 0) == 0

    def one(j, carry):
        for i, out_ref in enumerate((own_ref, other_ref)):
            t = NEED * i + j
            p = rows_of(pos, i)
            rows = pl.ds(pl.multiple_of(64 * (p % 4), 64), 64)
            total = None
            for kind in range(2):
                c = cos_ref[t, kind]
                s = sin_ref[t, kind]
                pieces = []
                for block in range(2):
                    cc, ss = c, s
                    if kind == 0 and block == 1:
                        cc = jnp.concatenate([jnp.where(top, nyq_ref[t, 0], c[:8]), c[8:]], axis=0)
                        ss = jnp.concatenate([jnp.where(top, nyq_ref[t, 1], s[:8]), s[8:]], axis=0)
                    lines = slice(QUART * block, QUART * block + QUART)
                    re, im = spec[kind, lines, :HALF], spec[kind, lines, HALF:]
                    pieces.append(jnp.concatenate([re * cc - im * ss, re * ss + im * cc], axis=1))
                part = dot3((b_ref[kind, 0, rows, :], b_ref[kind, 1, rows, :]), split(jnp.concatenate(pieces, axis=0)))
                total = part if kind == 0 else total + part * sign(p < 4)
            out_ref[j] = total
        return carry

    for j in range(NEED):
        one(j, 0)


def base_of(lower_ref, p):
    base = lower_ref[p, 0]
    for q in range(1, 8):
        base = jnp.minimum(base, lower_ref[p, q])
    return jnp.minimum(base, NREF - NEED)


def inverse_y(f, pos_ref, lower_ref, weight_ref, source_ref, table_ref, own_ref, came_ref, *refs):
    pos = pos_ref[0]
    core = pos % 2
    halves = []
    for kind, ref in ((core, own_ref), (1 - core, came_ref)):
        rows = [ref[j, :, HALF * c : HALF * c + HALF] for j in range(NEED) for c in range(2)]
        halves.append(dot3(split(jnp.concatenate(rows, axis=0)), (table_ref[kind, 0], table_ref[kind, 1])))
    flip = (1 - 2 * core).astype(F32)
    base = base_of(lower_ref, pos)
    lane = low_lanes((1, 128))
    coef = []
    for j in range(NEED):
        tiles = []
        for q in range(8):
            lower, weight = lower_ref[pos, q] - base, weight_ref[pos, q]
            tiles.append(jnp.where(lower == j, weight, 0.0) + jnp.where(lower + 1 == j, 1.0 - weight, 0.0))
        row = [jnp.where(lane, tiles[2 * t], tiles[2 * t + 1]) for t in range(4)]
        coef.append(row[:2] + [row[2] * flip, row[3] * flip])
    field = [[None] * 4, [None] * 4]
    for j in range(NEED):
        for c in range(2):
            rows = slice(128 * j + 64 * c, 128 * j + 64 * c + 64)
            for t in range(4):
                lanes = slice(128 * (t % 2), 128 * (t % 2) + 128)
                u, v = halves[0][rows, lanes], halves[1][rows, lanes]
                term = (u + v if t < 2 else u - v) * coef[j][t]
                field[c][t] = term if j == 0 else field[c][t] + term
    image = []
    for t in range(4):
        lanes = slice(128 * t, 128 * t + 128)
        image.append(field[0][t] * source_ref[f, :, 0, lanes] + field[1][t] * source_ref[f, :, 1, lanes])
    out_ref, image_ref = refs[:2] if f == 0 else refs[1:3]
    for t in range(4):
        lanes = slice(128 * t, 128 * t + 128)
        for c in range(2):
            out_ref[c, :, lanes] = field[c][t]
        if f == 0:
            image_ref[:, lanes] = image[t]
    if f == 0:
        return
    part_ref = refs[0]
    group = lax.broadcasted_iota(jnp.int32, (8, 128), 1) // 16
    for t in range(4):
        lanes = slice(128 * t, 128 * t + 128)
        total = (image[t] + part_ref[:, lanes]) * (1.0 / 8.0)
        cells = [total[8 * b : 8 * b + 8] for b in range(8)]
        for bit in (1, 2, 4):
            low = (group & bit) == 0
            new = [None] * 8
            for b in range(8):
                if b & bit:
                    continue
                x, y = cells[b], cells[b | bit]
                new[b] = jnp.where(low, x, pltpu.roll(y, 16 * bit, 1))
                new[b | bit] = jnp.where(low, pltpu.roll(x, 128 - 16 * bit, 1), y)
            cells = new
        for g in range(8):
            image_ref[8 * t + g] = cells[g]


def store_field(first_ref, second_ref, out_ref):
    for f, ref in enumerate((first_ref, second_ref)):
        for c in range(2):
            out_ref[f, :, c, :] = ref[c]


def sum_image(came_ref, out_ref):
    total = jnp.sum(came_ref[...], axis=0).T
    out_ref[0] = jnp.concatenate([total[16 * b : 16 * b + 16] for b in range(8)], axis=1)


VM = pl.BlockSpec(memory_space=pltpu.VMEM)
SM = pl.BlockSpec(memory_space=pltpu.SMEM)
HB = pl.BlockSpec(memory_space=pltpu.HBM)


def call(body, out, specs, scratch=(), f=None, grant=16):
    many = isinstance(out, (tuple, list))
    return pl.pallas_call(
        body if f is None else functools.partial(body, f),
        out_shape=out,
        in_specs=specs,
        out_specs=tuple(VM for _ in out) if many else VM,
        scratch_shapes=list(scratch),
        compiler_params=pltpu.CompilerParams(vmem_limit_bytes=grant * 2**20),
        interpret=INTERPRET,
    )


def shape(*dims):
    return jax.ShapeDtypeStruct(dims, F32)


def permute(values, chips, core=0):
    pairs = [(2 * x + c, 2 * ((x + chips) % 4) + (c + core) % 2) for x in range(4) for c in range(2)]
    return lax.ppermute(values, "pencil", pairs)


def whole(wave_field, source_field, omegas, velocities, lower_ref, blend_weight):
    pos = lax.axis_index("pencil").reshape(1)
    lower, weight = lower_ref[0], blend_weight[0]
    back, ahead = (jnp.asarray(t) for t in tables())
    out = call(
        forward_y,
        [shape(64, N)] * 4,
        [SM, HB, HB],
        [pltpu.VMEM(wave_field.shape, F32), pltpu.VMEM(back.shape, BF), pltpu.SemaphoreType.DMA((2,))],
        grant=FIRST,
    )(pos, *(pltpu.with_memory_space_constraint(x, pltpu.HBM) for x in (wave_field, back)))
    blocks, phase = [], []
    for f in range(2):
        here = (out[f], permute(out[2 + f], 0, 1))
        if f == 0:
            here = jnp.stack(here)
            right = permute(here, 1)
            left = permute(here, 3)
            held = (here, right, left)
        else:
            right = [permute(here[i], 1) for i in range(2)]
            left = [permute(here[i], 3) for i in range(2)]
            held = (*here, *right, *left)
        across = (permute(right[0], 1), permute(left[1], 3))
        blocks.append((*held, *across))
        phase.append(
            call(
                phases,
                [shape(2 * NEED, 2, QUART, HALF)] * 2 + [shape(2 * NEED, 2, 8, HALF)],
                [SM] * 4,
                [pltpu.VMEM((2, QUART, 128), F32)] * 2,
                f=f,
            )(pos, lower, omegas, velocities[0])
        )
    fields, images = [], []
    for f in range(2):
        mine, theirs = call(
            shift_x,
            [shape(NEED, 64, N)] * 2,
            [SM] + [VM] * (len(blocks[f]) + 5),
            [pltpu.VMEM((2, HALF, N), F32)] * 2,
            f,
        )(pos, *blocks[f], *phase[f], ahead, back)
        came = permute(theirs, 0, 1)
        field, image = call(
            inverse_y,
            [shape(2, 64, N), shape(64, N) if f == 0 else shape(32, 8, 128)],
            [SM] * 3 + [VM] * (4 + f),
            f=f,
        )(pos, lower, weight, source_field[0], ahead, mine, came, *images)
        fields.append(field)
        images.append(image)
    return finish(*fields, images[-1])


def finish(first, second, image):
    came = lax.all_to_all(image, "freq", 0, 0, tiled=True)
    field = call(store_field, shape(2, 64, 2, N), [VM] * 2)(first, second)
    image = call(sum_image, shape(1, 16, 64), [VM])(came)
    return field, jnp.transpose(image, (0, 2, 1))


def solution(mesh):
    placed = (
        P("freq", "pencil", None, None),
        P(None, "freq", "pencil", None, None),
        P("freq"),
        P(),
        P(),
        P(),
    )
    return jax.shard_map(
        whole,
        mesh=mesh,
        in_specs=placed,
        out_specs=(P("freq", "pencil", None, None), P(None, "pencil", "freq")),
        check_vma=False,
    )
```

profile of v0, /device:TPU:1, one launch (start us, length us, event | category | flops | bytes accessed | tf_op | source)
XLA Modules:
  0.0 58.8 jit_solution(10384747495418341852)
XLA Ops:
  0.6 0.0 copy-start.1
  0.6 0.0 copy-start
  0.7 0.0 copy-start.3
  0.7 1.7 %shard_map.95 = (f32[64,512]{1,0:T(8,128)S(1)}, f32[64,512]{1,0:T(8,128)S(1)}, f32[64,512]{1,0:T(8,128)S(1)}, f32[64,512]{1,0:T(8,128)S(1)}) custom-call(s32[1]{0:T(128)} %bitcast.pos_ref, f32[2,64,2,512]{3,2,1,0:T(2,128)} %wave_hbm.1, bf16[2,2,256,256]{3,2,1,0:T(8,128)(2,1)} %constant.8.clone.table_hbm.refs_9_.refs_12_), custom_call_target="tpu_custom_call" | custom-call | tf_op jit(solution)/shard_map/pallas_call | solution.py:306
  2.4 3.3 %collective-permute-start = (f32[64,512]{1,0:T(8,128)S(1)}, f32[64,512]{1,0:T(8,128)S(1)}, u32[]{:S(2)}, u32[]{:S(2)}) collective-permute-start(f32[64,512]{1,0:T(8,128)S(1)} %get-tuple-element.21), channel_id=1, source_target_pairs={{0,1},{1,0},{2,3},{3,2},{4,5},{5,4},{6,7},{7,6},{8,9},{9,8},{10,11... | collective-permute-start | bytes 393224 | tf_op jit(solution)/shard_map/ppermute | solution.py:299
  5.7 1.0 %collective-permute-done = f32[64,512]{1,0:T(8,128)S(1)} collective-permute-done((f32[64,512]{1,0:T(8,128)S(1)}, f32[64,512]{1,0:T(8,128)S(1)}, u32[]{:S(2)}, u32[]{:S(2)}) %collective-permute-start) | collective-permute-done | bytes 131104 | tf_op jit(solution)/shard_map/ppermute | solution.py:299
  6.7 0.1 collective-permute-start.1
  6.8 0.4 collective-permute-start.6
  7.3 2.9 %collective-permute-start.2 = (f32[2,64,512]{2,1,0:T(8,128)S(1)}, f32[2,64,512]{2,1,0:T(8,128)S(1)}, u32[]{:S(2)}, u32[]{:S(2)}) collective-permute-start(f32[2,64,512]{2,1,0:T(8,128)S(1)} %pad_maximum_fusion.refs_0_), channel_id=1, source_target_pairs={{0,6},{1,7},{2,0},{3,1},{4,2},{5,3},{6,4},{7,5},{8,14},{9,15},{10,... | collective-permute-start | bytes 786440 | tf_op jit(solution)/shard_map/ppermute | solution.py:299
  10.1 0.0 collective-permute-start.7
  10.1 0.0 collective-permute-done.6.refs_1_
  10.1 2.7 %collective-permute-start.10 = (f32[64,512]{1,0:T(8,128)S(1)}, f32[64,512]{1,0:T(8,128)S(1)}, u32[]{:S(2)}, u32[]{:S(2)}) collective-permute-start(f32[64,512]{1,0:T(8,128)S(1)} %collective-permute-done.6.refs_1_), channel_id=1, source_target_pairs={{0,6},{1,7},{2,0},{3,1},{4,2},{5,3},{6,4},{7,5},{8,14},{9,15},{10,... | collective-permute-start | bytes 393224 | tf_op jit(solution)/shard_map/ppermute | solution.py:299
  12.8 2.7 %collective-permute-done.1.refs_1_ = f32[2,64,512]{2,1,0:T(8,128)S(1)} collective-permute-done((f32[2,64,512]{2,1,0:T(8,128)S(1)}, f32[2,64,512]{2,1,0:T(8,128)S(1)}, u32[]{:S(2)}, u32[]{:S(2)}) %collective-permute-start.1) | collective-permute-done | bytes 262176 | tf_op jit(solution)/shard_map/ppermute | solution.py:299
  15.5 0.1 collective-permute-start.3
  15.6 0.2 collective-permute-done.2.refs_2_
  15.8 3.5 %collective-permute-start.4 = (f32[64,512]{1,0:T(8,128)S(1)}, f32[64,512]{1,0:T(8,128)S(1)}, u32[]{:S(2)}, u32[]{:S(2)}) collective-permute-start(f32[64,512]{1,0:T(8,128)S(1)} %slice_bitcast_fusion), channel_id=1, source_target_pairs={{0,6},{1,7},{2,0},{3,1},{4,2},{5,3},{6,4},{7,5},{8,14},{9,15},{10,... | collective-permute-start | bytes 393224 | tf_op jit(solution)/shard_map/ppermute | solution.py:299
  19.3 0.1 collective-permute-start.9
  19.4 0.0 collective-permute-done.7.refs_2_
  19.4 1.4 %collective-permute-start.8 = (f32[64,512]{1,0:T(8,128)S(1)}, f32[64,512]{1,0:T(8,128)S(1)}, u32[]{:S(2)}, u32[]{:S(2)}) collective-permute-start(f32[64,512]{1,0:T(8,128)S(1)} %collective-permute-done.6.refs_1_), channel_id=1, source_target_pairs={{0,2},{1,3},{2,4},{3,5},{4,6},{5,7},{6,0},{7,1},{8,10},{9,11},{10,... | collective-permute-start | bytes 393224 | tf_op jit(solution)/shard_map/ppermute | solution.py:299
  20.8 0.0 collective-permute-done.10.refs_5_
  20.8 0.1 collective-permute-start.11
  20.9 0.0 collective-permute-done.3.refs_3_
  20.9 2.6 %collective-permute-start.12 = (f32[64,512]{1,0:T(8,128)S(1)}, f32[64,512]{1,0:T(8,128)S(1)}, u32[]{:S(2)}, u32[]{:S(2)}) collective-permute-start(f32[64,512]{1,0:T(8,128)S(1)} %collective-permute-done.10.refs_5_), channel_id=1, source_target_pairs={{0,6},{1,7},{2,0},{3,1},{4,2},{5,3},{6,4},{7,5},{8,14},{9,15},{10,... | collective-permute-start | bytes 393224 | tf_op jit(solution)/shard_map/ppermute | solution.py:299
  23.5 0.0 copy-done.6
  23.5 2.0 %shard_map.96 = (f32[6,2,128,256]{3,2,1,0:T(8,128)S(1)}, f32[6,2,128,256]{3,2,1,0:T(8,128)S(1)}, f32[6,2,8,256]{3,2,1,0:T(8,128)S(1)}) custom-call(s32[1]{0:T(128)} %bitcast.pos_ref, s32[8,8]{1,0:T(8,128)S(1)} %bitcast.15, f32[2]{0:T(128)S(1)} %copy-done.5, f32[6]{0:T(128)S(1)} %bitcast.21), custom_call_target="tpu_custom_call" | custom-call | tf_op jit(solution)/shard_map/pallas_call | solution.py:328
  25.5 2.0 %shard_map.99 = (f32[6,2,128,256]{3,2,1,0:T(8,128)S(1)}, f32[6,2,128,256]{3,2,1,0:T(8,128)S(1)}, f32[6,2,8,256]{3,2,1,0:T(8,128)S(1)}) custom-call(s32[1]{0:T(128)} %bitcast.pos_ref, s32[8,8]{1,0:T(8,128)S(1)} %bitcast.16, f32[2]{0:T(128)S(1)} %copy-done.5, f32[6]{0:T(128)S(1)} %bitcast.22), custom_call_target="tpu_custom_call" | custom-call | tf_op jit(solution)/shard_map/pallas_call | solution.py:328
  27.6 0.0 collective-permute-done.4.refs_4_
  27.6 0.0 copy-done.1
  27.6 0.0 copy-done
  27.6 2.3 %shard_map.97 = (f32[3,64,512]{2,1,0:T(8,128)S(1)}, f32[3,64,512]{2,1,0:T(8,128)S(1)}) custom-call(s32[1]{0:T(128)} %bitcast.pos_ref, f32[2,64,512]{2,1,0:T(8,128)S(1)} %pad_maximum_fusion.refs_0_, f32[2,64,512]{2,1,0:T(8,128)S(1)} %collective-permute-done.1.refs_1_, f32[2,64,512]{2,1,0:T(8,128)S(1)} %collective-permute-done.2.refs_2_, ...), custom_call_target="tpu_custom_call" | custom-call | tf_op jit(solution)/shard_map/pallas_call | solution.py:338
  29.9 2.9 %collective-permute-start.5 = (f32[3,64,512]{2,1,0:T(8,128)S(1)}, f32[3,64,512]{2,1,0:T(8,128)S(1)}, u32[]{:S(2)}, u32[]{:S(2)}) collective-permute-start(f32[3,64,512]{2,1,0:T(8,128)S(1)} %get-tuple-element.26), channel_id=1, source_target_pairs={{0,1},{1,0},{2,3},{3,2},{4,5},{5,4},{6,7},{7,6},{8,9},{9,8},{10,11... | collective-permute-start | bytes 1179656 | tf_op jit(solution)/shard_map/ppermute | solution.py:299
  32.8 0.0 collective-permute-done.9.refs_4_
  32.8 0.0 collective-permute-done.8.refs_3_
  32.8 0.0 collective-permute-done.11.refs_6_
  32.8 0.0 collective-permute-done.12.refs_7_
  32.9 0.0 copy-start.2
  32.9 0.0 copy-start.4
  32.9 2.4 %shard_map.100 = (f32[3,64,512]{2,1,0:T(8,128)S(1)}, f32[3,64,512]{2,1,0:T(8,128)S(1)}) custom-call(s32[1]{0:T(128)} %bitcast.pos_ref, f32[64,512]{1,0:T(8,128)S(1)} %get-tuple-element.28.refs_0_, f32[64,512]{1,0:T(8,128)S(1)} %collective-permute-done.6.refs_1_, f32[64,512]{1,0:T(8,128)S(1)} %collective-permute-done.7.refs_2_, ...), custom_call_target="tpu_custom_call" | custom-call | tf_op jit(solution)/shard_map/pallas_call | solution.py:338
  35.3 0.1 collective-permute-start.13
  35.4 0.0 collective-permute-done.5.came_ref
  35.4 0.0 copy-done.2
  35.4 1.4 %shard_map.98 = (f32[2,64,512]{2,1,0:T(8,128)S(1)}, f32[64,512]{1,0:T(8,128)S(1)}) custom-call(s32[1]{0:T(128)} %bitcast.pos_ref, s32[8,8]{1,0:T(8,128)S(1)} %bitcast.17, f32[8,8]{1,0:T(8,128)S(1)} %bitcast.19, f32[2,64,2,512]{3,2,1,0:T(2,128)S(1)} %bitcast.12, bf16[2,2,256,256]{3,2,1,0:T(8,128)(2,1)S(1)} %copy-done, ...), custom_call_target="tpu_custom_call" | custom-call | tf_op jit(solution)/shard_map/pallas_call | solution.py:346
  36.8 0.3 collective-permute-done.13.came_ref
  37.1 2.3 %shard_map.101 = (f32[2,64,512]{2,1,0:T(8,128)S(1)}, f32[32,8,128]{2,1,0:T(8,128)}) custom-call(s32[1]{0:T(128)} %bitcast.pos_ref, s32[8,8]{1,0:T(8,128)S(1)} %bitcast.18, f32[8,8]{1,0:T(8,128)S(1)} %bitcast.20, f32[2,64,2,512]{3,2,1,0:T(2,128)S(1)} %bitcast.13, bf16[2,2,256,256]{3,2,1,0:T(8,128)(2,1)S(1)} %copy-done, ...), custom_call_target="tpu_custom_call" | custom-call | tf_op jit(solution)/shard_map/pallas_call | solution.py:346
  39.4 9.5 %all-to-all-start = ((f32[32,8,128]{2,1,0:T(8,128)}), f32[32,8,128]{2,1,0:T(8,128)S(1)}, u32[]{:S(2)}, u32[]{:S(2)}) async-start(f32[32,8,128]{2,1,0:T(8,128)} %get-tuple-element.37), calls=%async_computation | async-start | bytes 262144 | tf_op jit(solution)/shard_map/all_to_all | solution.py:358
  48.9 0.9 %shard_map.102 = f32[2,64,2,512]{3,2,1,0:T(2,128)} custom-call(f32[2,64,512]{2,1,0:T(8,128)S(1)} %get-tuple-element.27.first_ref, f32[2,64,512]{2,1,0:T(8,128)S(1)} %get-tuple-element.36.second_ref), custom_call_target="tpu_custom_call" | custom-call | tf_op jit(solution)/shard_map/pallas_call | solution.py:359
  49.8 8.3 %all-to-all-done.came_ref = f32[32,8,128]{2,1,0:T(8,128)S(1)} async-done(((f32[32,8,128]{2,1,0:T(8,128)}), f32[32,8,128]{2,1,0:T(8,128)S(1)}, u32[]{:S(2)}, u32[]{:S(2)}) %all-to-all-start) | async-done | bytes 131104 | tf_op jit(solution)/shard_map/all_to_all | solution.py:358
  58.0 0.8 %shard_map.103 = f32[1,16,64]{2,1,0:T(8,128)} custom-call(f32[32,8,128]{2,1,0:T(8,128)S(1)} %all-to-all-done.came_ref), custom_call_target="tpu_custom_call" | custom-call | tf_op jit(solution)/shard_map/pallas_call | solution.py:360
  (8 shorter events, 0.0 us)
Async XLA Ops:
  0.6 26.9 %copy-start.1 = (bf16[2,2,256,256]{3,2,1,0:T(8,128)(2,1)S(1)}, bf16[2,2,256,256]{3,2,1,0:T(8,128)(2,1)}, u32[]{:S(2)}) copy-start(bf16[2,2,256,256]{3,2,1,0:T(8,128)(2,1)} %constant.8.clone.table_hbm.refs_9_.refs_12_) | copy-start | bytes 1572868
  0.6 26.9 %copy-start = (bf16[2,2,256,256]{3,2,1,0:T(8,128)(2,1)S(1)}, bf16[2,2,256,256]{3,2,1,0:T(8,128)(2,1)}, u32[]{:S(2)}) copy-start(bf16[2,2,256,256]{3,2,1,0:T(8,128)(2,1)} %constant.9.clone.refs_8_.table_ref.refs_11_) | copy-start | bytes 1572868
  0.7 22.8 %copy-start.3 = (s32[1,8,8]{2,1,0:T(8,128)S(1)}, s32[1,8,8]{2,1,0:T(8,128)}, u32[]{:S(2)}) copy-start(s32[1,8,8]{2,1,0:T(8,128)} %param.12) | copy-start | bytes 772
  0.7 22.8 %copy-start.5 = (f32[2]{0:T(128)S(1)}, f32[2]{0:T(128)}, u32[]{:S(2)}) copy-start(f32[2]{0:T(128)} %omega_ref.3) | copy-start | bytes 28
  0.7 22.8 %copy-start.6 = (f32[1,6]{1,0:T(1,128)S(1)}, f32[1,6]{1,0:T(1,128)}, u32[]{:S(2)}) copy-start(f32[1,6]{1,0:T(1,128)} %param.11) | copy-start | bytes 76
  2.4 4.3 %collective-permute-start = (f32[64,512]{1,0:T(8,128)S(1)}, f32[64,512]{1,0:T(8,128)S(1)}, u32[]{:S(2)}, u32[]{:S(2)}) collective-permute-start(f32[64,512]{1,0:T(8,128)S(1)} %get-tuple-element.21), channel_id=1, source_target_pairs={{0,1},{1,0},{2,3},{3,2},{4,5},{5,4},{6,7},{7,6},{8,9},{9,8},{10,11... | collective-permute-start | bytes 393224 | tf_op jit(solution)/shard_map/ppermute | solution.py:299
  6.7 8.8 %collective-permute-start.1 = (f32[2,64,512]{2,1,0:T(8,128)S(1)}, f32[2,64,512]{2,1,0:T(8,128)S(1)}, u32[]{:S(2)}, u32[]{:S(2)}) collective-permute-start(f32[2,64,512]{2,1,0:T(8,128)S(1)} %pad_maximum_fusion.refs_0_), channel_id=1, source_target_pairs={{0,2},{1,3},{2,4},{3,5},{4,6},{5,7},{6,0},{7,1},{8,10},{9,11},{10,... | collective-permute-start | bytes 786440 | tf_op jit(solution)/shard_map/ppermute | solution.py:299
  6.8 3.3 %collective-permute-start.6 = (f32[64,512]{1,0:T(8,128)S(1)}, f32[64,512]{1,0:T(8,128)S(1)}, u32[]{:S(2)}, u32[]{:S(2)}) collective-permute-start(f32[64,512]{1,0:T(8,128)S(1)} %get-tuple-element.29), channel_id=1, source_target_pairs={{0,1},{1,0},{2,3},{3,2},{4,5},{5,4},{6,7},{7,6},{8,9},{9,8},{10,11... | collective-permute-start | bytes 393224 | tf_op jit(solution)/shard_map/ppermute | solution.py:299
  7.3 8.5 %collective-permute-start.2 = (f32[2,64,512]{2,1,0:T(8,128)S(1)}, f32[2,64,512]{2,1,0:T(8,128)S(1)}, u32[]{:S(2)}, u32[]{:S(2)}) collective-permute-start(f32[2,64,512]{2,1,0:T(8,128)S(1)} %pad_maximum_fusion.refs_0_), channel_id=1, source_target_pairs={{0,6},{1,7},{2,0},{3,1},{4,2},{5,3},{6,4},{7,5},{8,14},{9,15},{10,... | collective-permute-start | bytes 786440 | tf_op jit(solution)/shard_map/ppermute | solution.py:299
  10.1 9.3 %collective-permute-start.7 = (f32[64,512]{1,0:T(8,128)S(1)}, f32[64,512]{1,0:T(8,128)S(1)}, u32[]{:S(2)}, u32[]{:S(2)}) collective-permute-start(f32[64,512]{1,0:T(8,128)S(1)} %get-tuple-element.28.refs_0_), channel_id=1, source_target_pairs={{0,2},{1,3},{2,4},{3,5},{4,6},{5,7},{6,0},{7,1},{8,10},{9,11},{10,... | collective-permute-start | bytes 393224 | tf_op jit(solution)/shard_map/ppermute | solution.py:299
  10.1 10.6 %collective-permute-start.10 = (f32[64,512]{1,0:T(8,128)S(1)}, f32[64,512]{1,0:T(8,128)S(1)}, u32[]{:S(2)}, u32[]{:S(2)}) collective-permute-start(f32[64,512]{1,0:T(8,128)S(1)} %collective-permute-done.6.refs_1_), channel_id=1, source_target_pairs={{0,6},{1,7},{2,0},{3,1},{4,2},{5,3},{6,4},{7,5},{8,14},{9,15},{10,... | collective-permute-start | bytes 393224 | tf_op jit(solution)/shard_map/ppermute | solution.py:299
  15.5 5.3 %collective-permute-start.3 = (f32[64,512]{1,0:T(8,128)S(1)}, f32[64,512]{1,0:T(8,128)S(1)}, u32[]{:S(2)}, u32[]{:S(2)}) collective-permute-start(f32[64,512]{1,0:T(8,128)S(1)} %slice_bitcast_fusion.1), channel_id=1, source_target_pairs={{0,2},{1,3},{2,4},{3,5},{4,6},{5,7},{6,0},{7,1},{8,10},{9,11},{10,... | collective-permute-start | bytes 393224 | tf_op jit(solution)/shard_map/ppermute | solution.py:299
  15.8 11.8 %collective-permute-start.4 = (f32[64,512]{1,0:T(8,128)S(1)}, f32[64,512]{1,0:T(8,128)S(1)}, u32[]{:S(2)}, u32[]{:S(2)}) collective-permute-start(f32[64,512]{1,0:T(8,128)S(1)} %slice_bitcast_fusion), channel_id=1, source_target_pairs={{0,6},{1,7},{2,0},{3,1},{4,2},{5,3},{6,4},{7,5},{8,14},{9,15},{10,... | collective-permute-start | bytes 393224 | tf_op jit(solution)/shard_map/ppermute | solution.py:299
  19.3 13.5 %collective-permute-start.9 = (f32[64,512]{1,0:T(8,128)S(1)}, f32[64,512]{1,0:T(8,128)S(1)}, u32[]{:S(2)}, u32[]{:S(2)}) collective-permute-start(f32[64,512]{1,0:T(8,128)S(1)} %get-tuple-element.28.refs_0_), channel_id=1, source_target_pairs={{0,6},{1,7},{2,0},{3,1},{4,2},{5,3},{6,4},{7,5},{8,14},{9,15},{10,... | collective-permute-start | bytes 393224 | tf_op jit(solution)/shard_map/ppermute | solution.py:299
  19.4 13.4 %collective-permute-start.8 = (f32[64,512]{1,0:T(8,128)S(1)}, f32[64,512]{1,0:T(8,128)S(1)}, u32[]{:S(2)}, u32[]{:S(2)}) collective-permute-start(f32[64,512]{1,0:T(8,128)S(1)} %collective-permute-done.6.refs_1_), channel_id=1, source_target_pairs={{0,2},{1,3},{2,4},{3,5},{4,6},{5,7},{6,0},{7,1},{8,10},{9,11},{10,... | collective-permute-start | bytes 393224 | tf_op jit(solution)/shard_map/ppermute | solution.py:299
  20.8 12.1 %collective-permute-start.11 = (f32[64,512]{1,0:T(8,128)S(1)}, f32[64,512]{1,0:T(8,128)S(1)}, u32[]{:S(2)}, u32[]{:S(2)}) collective-permute-start(f32[64,512]{1,0:T(8,128)S(1)} %collective-permute-done.7.refs_2_), channel_id=1, source_target_pairs={{0,2},{1,3},{2,4},{3,5},{4,6},{5,7},{6,0},{7,1},{8,10},{9,11},{10,... | collective-permute-start | bytes 393224 | tf_op jit(solution)/shard_map/ppermute | solution.py:299
  20.9 12.0 %collective-permute-start.12 = (f32[64,512]{1,0:T(8,128)S(1)}, f32[64,512]{1,0:T(8,128)S(1)}, u32[]{:S(2)}, u32[]{:S(2)}) collective-permute-start(f32[64,512]{1,0:T(8,128)S(1)} %collective-permute-done.10.refs_5_), channel_id=1, source_target_pairs={{0,6},{1,7},{2,0},{3,1},{4,2},{5,3},{6,4},{7,5},{8,14},{9,15},{10,... | collective-permute-start | bytes 393224 | tf_op jit(solution)/shard_map/ppermute | solution.py:299
  29.9 5.5 %collective-permute-start.5 = (f32[3,64,512]{2,1,0:T(8,128)S(1)}, f32[3,64,512]{2,1,0:T(8,128)S(1)}, u32[]{:S(2)}, u32[]{:S(2)}) collective-permute-start(f32[3,64,512]{2,1,0:T(8,128)S(1)} %get-tuple-element.26), channel_id=1, source_target_pairs={{0,1},{1,0},{2,3},{3,2},{4,5},{5,4},{6,7},{7,6},{8,9},{9,8},{10,11... | collective-permute-start | bytes 1179656 | tf_op jit(solution)/shard_map/ppermute | solution.py:299
  32.9 2.6 %copy-start.2 = (f32[1,2,64,2,512]{4,3,2,1,0:T(2,128)S(1)}, f32[1,2,64,2,512]{4,3,2,1,0:T(2,128)}, u32[]{:S(2)}) copy-start(f32[1,2,64,2,512]{4,3,2,1,0:T(2,128)} %param.9) | copy-start | bytes 1572868
  32.9 2.6 %copy-start.4 = (f32[1,8,8]{2,1,0:T(8,128)S(1)}, f32[1,8,8]{2,1,0:T(8,128)}, u32[]{:S(2)}) copy-start(f32[1,8,8]{2,1,0:T(8,128)} %param.13) | copy-start | bytes 772
  35.3 1.8 %collective-permute-start.13 = (f32[3,64,512]{2,1,0:T(8,128)S(1)}, f32[3,64,512]{2,1,0:T(8,128)S(1)}, u32[]{:S(2)}, u32[]{:S(2)}) collective-permute-start(f32[3,64,512]{2,1,0:T(8,128)S(1)} %get-tuple-element.34), channel_id=1, source_target_pairs={{0,1},{1,0},{2,3},{3,2},{4,5},{5,4},{6,7},{7,6},{8,9},{9,8},{10,11... | collective-permute-start | bytes 1179656 | tf_op jit(solution)/shard_map/ppermute | solution.py:299
  39.4 18.7 %all-to-all-start = ((f32[32,8,128]{2,1,0:T(8,128)}), f32[32,8,128]{2,1,0:T(8,128)S(1)}, u32[]{:S(2)}, u32[]{:S(2)}) async-start(f32[32,8,128]{2,1,0:T(8,128)} %get-tuple-element.37), calls=%async_computation | async-start | bytes 262144 | tf_op jit(solution)/shard_map/all_to_all | solution.py:358
where the time goes:
time: 59 us; the launch traced here: 58.8 us
  starting transfers between devices  29.6 us (50%)
  Pallas kernels  15.9 us (27%)
  waiting for transfers between devices  12.4 us (21%)
  between operations  0.82 us (1%)
    ppermute x14, starting transfers between devices, permute(): return lax.ppermute(values, 'pencil', pairs)  20.1 us
    all_to_all x1, starting transfers between devices, finish(): came = lax.all_to_all(image, 'freq', 0, 0, tiled=True)  9.49 us
    all_to_all x1, waiting for transfers between devices, finish(): came = lax.all_to_all(image, 'freq', 0, 0, tiled=True)  8.26 us
    pallas_call x2, Pallas kernels, whole(): call(shift_x, [shape(NEED, 64, N)] * 2, [SM] + [VM] * (len(blocks[f]) + 5...  4.76 us
    ppermute x14, waiting for transfers between devices, permute(): return lax.ppermute(values, 'pencil', pairs)  4.18 us
    pallas_call x2, Pallas kernels, whole(): call(phases, [shape(2 * NEED, 2, QUART, HALF)] * 2 + [shape(2 * NEED, 2,...  4.09 us
    pallas_call x2, Pallas kernels, whole(): call(inverse_y, [shape(2, 64, N), shape(64, N) if f == 0 else shape(32, 8...  3.63 us
    pallas_call x1, Pallas kernels, whole(): call(forward_y, [shape(64, N)] * 4, [SM, HB, HB], [pltpu.VMEM(wave_field....  1.74 us
  transfers between devices with their start and end apart: 15, of which 5 were waited for; matrix products, arithmetic and copies ran while one was open for 0% of the time, Pallas kernels for 19%

commit v1 on v0

--- a/solution.py
+++ b/solution.py
@@ -233,15 +233,15 @@
         lanes = slice(128 * t, 128 * t + 128)
         image.append(field[0][t] * source_ref[f, :, 0, lanes] + field[1][t] * source_ref[f, :, 1, lanes])
     out_ref, image_ref = refs[:2] if f == 0 else refs[1:3]
-    for t in range(4):
-        lanes = slice(128 * t, 128 * t + 128)
-        for c in range(2):
-            out_ref[c, :, lanes] = field[c][t]
-        if f == 0:
+    if f == 0:
+        for t in range(4):
+            lanes = slice(128 * t, 128 * t + 128)
             image_ref[:, lanes] = image[t]
-    if f == 0:
+            for c in range(2):
+                out_ref[c, :, lanes] = field[c][t]
         return
-    part_ref = refs[0]
+    part_ref, (packed, sem) = refs[0], refs[3:]
+    copies = []
     group = lax.broadcasted_iota(jnp.int32, (8, 128), 1) // 16
     for t in range(4):
         lanes = slice(128 * t, 128 * t + 128)
@@ -258,7 +258,16 @@
                 new[b | bit] = jnp.where(low, pltpu.roll(x, 128 - 16 * bit, 1), y)
             cells = new
         for g in range(8):
-            image_ref[8 * t + g] = cells[g]
+            packed[8 * t + g] = cells[g]
+        rows = pl.ds(8 * t, 8)
+        copies.append(pltpu.make_async_copy(packed.at[rows], image_ref.at[rows], sem.at[t]))
+        copies[t].start()
+    for t in range(4):
+        lanes = slice(128 * t, 128 * t + 128)
+        for c in range(2):
+            out_ref[c, :, lanes] = field[c][t]
+    for copy in copies:
+        copy.wait()
 
 
 def store_field(first_ref, second_ref, out_ref):
@@ -277,13 +286,13 @@
 HB = pl.BlockSpec(memory_space=pltpu.HBM)
 
 
-def call(body, out, specs, scratch=(), f=None, grant=16):
+def call(body, out, specs, scratch=(), f=None, grant=16, outs=None):
     many = isinstance(out, (tuple, list))
     return pl.pallas_call(
         body if f is None else functools.partial(body, f),
         out_shape=out,
         in_specs=specs,
-        out_specs=tuple(VM for _ in out) if many else VM,
+        out_specs=outs or (tuple(VM for _ in out) if many else VM),
         scratch_shapes=list(scratch),
         compiler_params=pltpu.CompilerParams(vmem_limit_bytes=grant * 2**20),
         interpret=INTERPRET,
@@ -347,7 +356,9 @@
             inverse_y,
             [shape(2, 64, N), shape(64, N) if f == 0 else shape(32, 8, 128)],
             [SM] * 3 + [VM] * (4 + f),
+            [pltpu.VMEM((32, 8, 128), F32), pltpu.SemaphoreType.DMA((4,))] if f else [],
             f=f,
+            outs=(VM, HB) if f else None,
         )(pos, lower, weight, source_field[0], ahead, mine, came, *images)
         fields.append(field)
         images.append(image)

time: 59 us -> 59.1 us (level)
  no operation moved by 1% of the time
where the time goes in v1:
time: 59.1 us; the launch traced here: 58.9 us
  starting transfers between devices  29.6 us (50%)
  Pallas kernels  15.9 us (27%)
  waiting for transfers between devices  12.4 us (21%)
  between operations  0.83 us (1%)
    ppermute x14, starting transfers between devices, permute(): return lax.ppermute(values, 'pencil', pairs)  20.1 us
    all_to_all x1, starting transfers between devices, finish(): came = lax.all_to_all(image, 'freq', 0, 0, tiled=True)  9.5 us
    all_to_all x1, waiting for transfers between devices, finish(): came = lax.all_to_all(image, 'freq', 0, 0, tiled=True)  8.26 us
    pallas_call x2, Pallas kernels, whole(): call(shift_x, [shape(NEED, 64, N)] * 2, [SM] + [VM] * (len(blocks[f]) + 5...  4.76 us
    ppermute x14, waiting for transfers between devices, permute(): return lax.ppermute(values, 'pencil', pairs)  4.18 us
    pallas_call x2, Pallas kernels, whole(): call(phases, [shape(2 * NEED, 2, QUART, HALF)] * 2 + [shape(2 * NEED, 2,...  4.09 us
    pallas_call x2, Pallas kernels, whole(): call(inverse_y, [shape(2, 64, N), shape(64, N) if f == 0 else shape(32, 8...  3.66 us
    pallas_call x1, Pallas kernels, whole(): call(forward_y, [shape(64, N)] * 4, [SM, HB, HB], [pltpu.VMEM(wave_field....  1.74 us
  transfers between devices with their start and end apart: 15, of which 5 were waited for; matrix products, arithmetic and copies ran while one was open for 0% of the time, Pallas kernels for 19%

profile of v1, /device:TPU:1, one launch (start us, length us, event | category | flops | bytes accessed | tf_op | source)
XLA Modules:
  0.0 58.9 jit_solution(6238722075497723257)
XLA Ops:
  0.6 0.0 copy-start.1
  0.6 0.0 copy-start
  0.7 0.0 copy-start.3
  0.7 1.7 %shard_map.95 = (f32[64,512]{1,0:T(8,128)S(1)}, f32[64,512]{1,0:T(8,128)S(1)}, f32[64,512]{1,0:T(8,128)S(1)}, f32[64,512]{1,0:T(8,128)S(1)}) custom-call(s32[1]{0:T(128)} %bitcast.pos_ref, f32[2,64,2,512]{3,2,1,0:T(2,128)} %wave_hbm.1, bf16[2,2,256,256]{3,2,1,0:T(8,128)(2,1)} %constant.8.clone.table_hbm.refs_9_.refs_12_), custom_call_target="tpu_custom_call" | custom-call | tf_op jit(solution)/shard_map/pallas_call | solution.py:315
  2.4 3.3 %collective-permute-start = (f32[64,512]{1,0:T(8,128)S(1)}, f32[64,512]{1,0:T(8,128)S(1)}, u32[]{:S(2)}, u32[]{:S(2)}) collective-permute-start(f32[64,512]{1,0:T(8,128)S(1)} %get-tuple-element.21), channel_id=1, source_target_pairs={{0,1},{1,0},{2,3},{3,2},{4,5},{5,4},{6,7},{7,6},{8,9},{9,8},{10,11... | collective-permute-start | bytes 393224 | tf_op jit(solution)/shard_map/ppermute | solution.py:308
  5.7 1.0 %collective-permute-done = f32[64,512]{1,0:T(8,128)S(1)} collective-permute-done((f32[64,512]{1,0:T(8,128)S(1)}, f32[64,512]{1,0:T(8,128)S(1)}, u32[]{:S(2)}, u32[]{:S(2)}) %collective-permute-start) | collective-permute-done | bytes 131104 | tf_op jit(solution)/shard_map/ppermute | solution.py:308
  6.7 0.1 collective-permute-start.1
  6.8 0.4 collective-permute-start.6
  7.3 2.9 %collective-permute-start.2 = (f32[2,64,512]{2,1,0:T(8,128)S(1)}, f32[2,64,512]{2,1,0:T(8,128)S(1)}, u32[]{:S(2)}, u32[]{:S(2)}) collective-permute-start(f32[2,64,512]{2,1,0:T(8,128)S(1)} %pad_maximum_fusion.refs_0_), channel_id=1, source_target_pairs={{0,6},{1,7},{2,0},{3,1},{4,2},{5,3},{6,4},{7,5},{8,14},{9,15},{10,... | collective-permute-start | bytes 786440 | tf_op jit(solution)/shard_map/ppermute | solution.py:308
  10.1 0.0 collective-permute-start.7
  10.1 0.0 collective-permute-done.6.refs_1_
  10.1 2.7 %collective-permute-start.10 = (f32[64,512]{1,0:T(8,128)S(1)}, f32[64,512]{1,0:T(8,128)S(1)}, u32[]{:S(2)}, u32[]{:S(2)}) collective-permute-start(f32[64,512]{1,0:T(8,128)S(1)} %collective-permute-done.6.refs_1_), channel_id=1, source_target_pairs={{0,6},{1,7},{2,0},{3,1},{4,2},{5,3},{6,4},{7,5},{8,14},{9,15},{10,... | collective-permute-start | bytes 393224 | tf_op jit(solution)/shard_map/ppermute | solution.py:308
  12.8 2.7 %collective-permute-done.1.refs_1_ = f32[2,64,512]{2,1,0:T(8,128)S(1)} collective-permute-done((f32[2,64,512]{2,1,0:T(8,128)S(1)}, f32[2,64,512]{2,1,0:T(8,128)S(1)}, u32[]{:S(2)}, u32[]{:S(2)}) %collective-permute-start.1) | collective-permute-done | bytes 262176 | tf_op jit(solution)/shard_map/ppermute | solution.py:308
  15.5 0.1 collective-permute-start.3
  15.6 0.2 collective-permute-done.2.refs_2_
  15.8 3.5 %collective-permute-start.4 = (f32[64,512]{1,0:T(8,128)S(1)}, f32[64,512]{1,0:T(8,128)S(1)}, u32[]{:S(2)}, u32[]{:S(2)}) collective-permute-start(f32[64,512]{1,0:T(8,128)S(1)} %slice_bitcast_fusion), channel_id=1, source_target_pairs={{0,6},{1,7},{2,0},{3,1},{4,2},{5,3},{6,4},{7,5},{8,14},{9,15},{10,... | collective-permute-start | bytes 393224 | tf_op jit(solution)/shard_map/ppermute | solution.py:308
  19.3 0.1 collective-permute-start.9
  19.4 0.0 collective-permute-done.7.refs_2_
  19.4 1.4 %collective-permute-start.8 = (f32[64,512]{1,0:T(8,128)S(1)}, f32[64,512]{1,0:T(8,128)S(1)}, u32[]{:S(2)}, u32[]{:S(2)}) collective-permute-start(f32[64,512]{1,0:T(8,128)S(1)} %collective-permute-done.6.refs_1_), channel_id=1, source_target_pairs={{0,2},{1,3},{2,4},{3,5},{4,6},{5,7},{6,0},{7,1},{8,10},{9,11},{10,... | collective-permute-start | bytes 393224 | tf_op jit(solution)/shard_map/ppermute | solution.py:308
  20.8 0.0 collective-permute-done.10.refs_5_
  20.8 0.1 collective-permute-start.11
  20.9 0.0 collective-permute-done.3.refs_3_
  20.9 2.6 %collective-permute-start.12 = (f32[64,512]{1,0:T(8,128)S(1)}, f32[64,512]{1,0:T(8,128)S(1)}, u32[]{:S(2)}, u32[]{:S(2)}) collective-permute-start(f32[64,512]{1,0:T(8,128)S(1)} %collective-permute-done.10.refs_5_), channel_id=1, source_target_pairs={{0,6},{1,7},{2,0},{3,1},{4,2},{5,3},{6,4},{7,5},{8,14},{9,15},{10,... | collective-permute-start | bytes 393224 | tf_op jit(solution)/shard_map/ppermute | solution.py:308
  23.5 0.0 copy-done.6
  23.5 2.0 %shard_map.96 = (f32[6,2,128,256]{3,2,1,0:T(8,128)S(1)}, f32[6,2,128,256]{3,2,1,0:T(8,128)S(1)}, f32[6,2,8,256]{3,2,1,0:T(8,128)S(1)}) custom-call(s32[1]{0:T(128)} %bitcast.pos_ref, s32[8,8]{1,0:T(8,128)S(1)} %bitcast.15, f32[2]{0:T(128)S(1)} %copy-done.5, f32[6]{0:T(128)S(1)} %bitcast.21), custom_call_target="tpu_custom_call" | custom-call | tf_op jit(solution)/shard_map/pallas_call | solution.py:337
  25.5 2.0 %shard_map.99 = (f32[6,2,128,256]{3,2,1,0:T(8,128)S(1)}, f32[6,2,128,256]{3,2,1,0:T(8,128)S(1)}, f32[6,2,8,256]{3,2,1,0:T(8,128)S(1)}) custom-call(s32[1]{0:T(128)} %bitcast.pos_ref, s32[8,8]{1,0:T(8,128)S(1)} %bitcast.16, f32[2]{0:T(128)S(1)} %copy-done.5, f32[6]{0:T(128)S(1)} %bitcast.22), custom_call_target="tpu_custom_call" | custom-call | tf_op jit(solution)/shard_map/pallas_call | solution.py:337
  27.6 0.0 collective-permute-done.4.refs_4_
  27.6 0.0 copy-done.1
  27.6 0.0 copy-done
  27.6 2.3 %shard_map.97 = (f32[3,64,512]{2,1,0:T(8,128)S(1)}, f32[3,64,512]{2,1,0:T(8,128)S(1)}) custom-call(s32[1]{0:T(128)} %bitcast.pos_ref, f32[2,64,512]{2,1,0:T(8,128)S(1)} %pad_maximum_fusion.refs_0_, f32[2,64,512]{2,1,0:T(8,128)S(1)} %collective-permute-done.1.refs_1_, f32[2,64,512]{2,1,0:T(8,128)S(1)} %collective-permute-done.2.refs_2_, ...), custom_call_target="tpu_custom_call" | custom-call | tf_op jit(solution)/shard_map/pallas_call | solution.py:347
  29.9 2.9 %collective-permute-start.5 = (f32[3,64,512]{2,1,0:T(8,128)S(1)}, f32[3,64,512]{2,1,0:T(8,128)S(1)}, u32[]{:S(2)}, u32[]{:S(2)}) collective-permute-start(f32[3,64,512]{2,1,0:T(8,128)S(1)} %get-tuple-element.26), channel_id=1, source_target_pairs={{0,1},{1,0},{2,3},{3,2},{4,5},{5,4},{6,7},{7,6},{8,9},{9,8},{10,11... | collective-permute-start | bytes 1179656 | tf_op jit(solution)/shard_map/ppermute | solution.py:308
  32.8 0.0 collective-permute-done.9.refs_4_
  32.8 0.0 collective-permute-done.8.refs_3_
  32.8 0.0 collective-permute-done.11.refs_6_
  32.8 0.0 collective-permute-done.12.refs_7_
  32.9 0.0 copy-start.2
  32.9 0.0 copy-start.4
  32.9 2.4 %shard_map.100 = (f32[3,64,512]{2,1,0:T(8,128)S(1)}, f32[3,64,512]{2,1,0:T(8,128)S(1)}) custom-call(s32[1]{0:T(128)} %bitcast.pos_ref, f32[64,512]{1,0:T(8,128)S(1)} %get-tuple-element.28.refs_0_, f32[64,512]{1,0:T(8,128)S(1)} %collective-permute-done.6.refs_1_, f32[64,512]{1,0:T(8,128)S(1)} %collective-permute-done.7.refs_2_, ...), custom_call_target="tpu_custom_call" | custom-call | tf_op jit(solution)/shard_map/pallas_call | solution.py:347
  35.3 0.1 collective-permute-start.13
  35.4 0.0 collective-permute-done.5.came_ref
  35.4 0.0 copy-done.2
  35.4 1.4 %shard_map.98 = (f32[2,64,512]{2,1,0:T(8,128)S(1)}, f32[64,512]{1,0:T(8,128)S(1)}) custom-call(s32[1]{0:T(128)} %bitcast.pos_ref, s32[8,8]{1,0:T(8,128)S(1)} %bitcast.17, f32[8,8]{1,0:T(8,128)S(1)} %bitcast.19, f32[2,64,2,512]{3,2,1,0:T(2,128)S(1)} %bitcast.12, bf16[2,2,256,256]{3,2,1,0:T(8,128)(2,1)S(1)} %copy-done, ...), custom_call_target="tpu_custom_call" | custom-call | tf_op jit(solution)/shard_map/pallas_call | solution.py:355
  36.8 0.3 collective-permute-done.13.came_ref
  37.1 2.3 %shard_map.101 = (f32[2,64,512]{2,1,0:T(8,128)S(1)}, f32[32,8,128]{2,1,0:T(8,128)}) custom-call(s32[1]{0:T(128)} %bitcast.pos_ref, s32[8,8]{1,0:T(8,128)S(1)} %bitcast.18, f32[8,8]{1,0:T(8,128)S(1)} %bitcast.20, f32[2,64,2,512]{3,2,1,0:T(2,128)S(1)} %bitcast.13, bf16[2,2,256,256]{3,2,1,0:T(8,128)(2,1)S(1)} %copy-done, ...), custom_call_target="tpu_custom_call" | custom-call | tf_op jit(solution)/shard_map/pallas_call | solution.py:355
  39.4 9.5 %all-to-all-start = ((f32[32,8,128]{2,1,0:T(8,128)}), f32[32,8,128]{2,1,0:T(8,128)S(1)}, u32[]{:S(2)}, u32[]{:S(2)}) async-start(f32[32,8,128]{2,1,0:T(8,128)} %get-tuple-element.37), calls=%async_computation | async-start | bytes 262144 | tf_op jit(solution)/shard_map/all_to_all | solution.py:369
  48.9 0.9 %shard_map.102 = f32[2,64,2,512]{3,2,1,0:T(2,128)} custom-call(f32[2,64,512]{2,1,0:T(8,128)S(1)} %get-tuple-element.27.first_ref, f32[2,64,512]{2,1,0:T(8,128)S(1)} %get-tuple-element.36.second_ref), custom_call_target="tpu_custom_call" | custom-call | tf_op jit(solution)/shard_map/pallas_call | solution.py:370
  49.8 8.3 %all-to-all-done.came_ref = f32[32,8,128]{2,1,0:T(8,128)S(1)} async-done(((f32[32,8,128]{2,1,0:T(8,128)}), f32[32,8,128]{2,1,0:T(8,128)S(1)}, u32[]{:S(2)}, u32[]{:S(2)}) %all-to-all-start) | async-done | bytes 131104 | tf_op jit(solution)/shard_map/all_to_all | solution.py:369
  58.1 0.8 %shard_map.103 = f32[1,16,64]{2,1,0:T(8,128)} custom-call(f32[32,8,128]{2,1,0:T(8,128)S(1)} %all-to-all-done.came_ref), custom_call_target="tpu_custom_call" | custom-call | tf_op jit(solution)/shard_map/pallas_call | solution.py:371
  (8 shorter events, 0.0 us)
Async XLA Ops:
  0.6 26.9 %copy-start.1 = (bf16[2,2,256,256]{3,2,1,0:T(8,128)(2,1)S(1)}, bf16[2,2,256,256]{3,2,1,0:T(8,128)(2,1)}, u32[]{:S(2)}) copy-start(bf16[2,2,256,256]{3,2,1,0:T(8,128)(2,1)} %constant.8.clone.table_hbm.refs_9_.refs_12_) | copy-start | bytes 1572868
  0.6 26.9 %copy-start = (bf16[2,2,256,256]{3,2,1,0:T(8,128)(2,1)S(1)}, bf16[2,2,256,256]{3,2,1,0:T(8,128)(2,1)}, u32[]{:S(2)}) copy-start(bf16[2,2,256,256]{3,2,1,0:T(8,128)(2,1)} %constant.9.clone.refs_8_.table_ref.refs_11_) | copy-start | bytes 1572868
  0.7 22.8 %copy-start.3 = (s32[1,8,8]{2,1,0:T(8,128)S(1)}, s32[1,8,8]{2,1,0:T(8,128)}, u32[]{:S(2)}) copy-start(s32[1,8,8]{2,1,0:T(8,128)} %param.12) | copy-start | bytes 772
  0.7 22.8 %copy-start.5 = (f32[2]{0:T(128)S(1)}, f32[2]{0:T(128)}, u32[]{:S(2)}) copy-start(f32[2]{0:T(128)} %omega_ref.3) | copy-start | bytes 28
  0.7 22.8 %copy-start.6 = (f32[1,6]{1,0:T(1,128)S(1)}, f32[1,6]{1,0:T(1,128)}, u32[]{:S(2)}) copy-start(f32[1,6]{1,0:T(1,128)} %param.11) | copy-start | bytes 76
  2.4 4.3 %collective-permute-start = (f32[64,512]{1,0:T(8,128)S(1)}, f32[64,512]{1,0:T(8,128)S(1)}, u32[]{:S(2)}, u32[]{:S(2)}) collective-permute-start(f32[64,512]{1,0:T(8,128)S(1)} %get-tuple-element.21), channel_id=1, source_target_pairs={{0,1},{1,0},{2,3},{3,2},{4,5},{5,4},{6,7},{7,6},{8,9},{9,8},{10,11... | collective-permute-start | bytes 393224 | tf_op jit(solution)/shard_map/ppermute | solution.py:308
  6.7 8.8 %collective-permute-start.1 = (f32[2,64,512]{2,1,0:T(8,128)S(1)}, f32[2,64,512]{2,1,0:T(8,128)S(1)}, u32[]{:S(2)}, u32[]{:S(2)}) collective-permute-start(f32[2,64,512]{2,1,0:T(8,128)S(1)} %pad_maximum_fusion.refs_0_), channel_id=1, source_target_pairs={{0,2},{1,3},{2,4},{3,5},{4,6},{5,7},{6,0},{7,1},{8,10},{9,11},{10,... | collective-permute-start | bytes 786440 | tf_op jit(solution)/shard_map/ppermute | solution.py:308
  6.8 3.3 %collective-permute-start.6 = (f32[64,512]{1,0:T(8,128)S(1)}, f32[64,512]{1,0:T(8,128)S(1)}, u32[]{:S(2)}, u32[]{:S(2)}) collective-permute-start(f32[64,512]{1,0:T(8,128)S(1)} %get-tuple-element.29), channel_id=1, source_target_pairs={{0,1},{1,0},{2,3},{3,2},{4,5},{5,4},{6,7},{7,6},{8,9},{9,8},{10,11... | collective-permute-start | bytes 393224 | tf_op jit(solution)/shard_map/ppermute | solution.py:308
  7.3 8.5 %collective-permute-start.2 = (f32[2,64,512]{2,1,0:T(8,128)S(1)}, f32[2,64,512]{2,1,0:T(8,128)S(1)}, u32[]{:S(2)}, u32[]{:S(2)}) collective-permute-start(f32[2,64,512]{2,1,0:T(8,128)S(1)} %pad_maximum_fusion.refs_0_), channel_id=1, source_target_pairs={{0,6},{1,7},{2,0},{3,1},{4,2},{5,3},{6,4},{7,5},{8,14},{9,15},{10,... | collective-permute-start | bytes 786440 | tf_op jit(solution)/shard_map/ppermute | solution.py:308
  10.1 9.3 %collective-permute-start.7 = (f32[64,512]{1,0:T(8,128)S(1)}, f32[64,512]{1,0:T(8,128)S(1)}, u32[]{:S(2)}, u32[]{:S(2)}) collective-permute-start(f32[64,512]{1,0:T(8,128)S(1)} %get-tuple-element.28.refs_0_), channel_id=1, source_target_pairs={{0,2},{1,3},{2,4},{3,5},{4,6},{5,7},{6,0},{7,1},{8,10},{9,11},{10,... | collective-permute-start | bytes 393224 | tf_op jit(solution)/shard_map/ppermute | solution.py:308
  10.1 10.6 %collective-permute-start.10 = (f32[64,512]{1,0:T(8,128)S(1)}, f32[64,512]{1,0:T(8,128)S(1)}, u32[]{:S(2)}, u32[]{:S(2)}) collective-permute-start(f32[64,512]{1,0:T(8,128)S(1)} %collective-permute-done.6.refs_1_), channel_id=1, source_target_pairs={{0,6},{1,7},{2,0},{3,1},{4,2},{5,3},{6,4},{7,5},{8,14},{9,15},{10,... | collective-permute-start | bytes 393224 | tf_op jit(solution)/shard_map/ppermute | solution.py:308
  15.5 5.3 %collective-permute-start.3 = (f32[64,512]{1,0:T(8,128)S(1)}, f32[64,512]{1,0:T(8,128)S(1)}, u32[]{:S(2)}, u32[]{:S(2)}) collective-permute-start(f32[64,512]{1,0:T(8,128)S(1)} %slice_bitcast_fusion.1), channel_id=1, source_target_pairs={{0,2},{1,3},{2,4},{3,5},{4,6},{5,7},{6,0},{7,1},{8,10},{9,11},{10,... | collective-permute-start | bytes 393224 | tf_op jit(solution)/shard_map/ppermute | solution.py:308
  15.8 11.8 %collective-permute-start.4 = (f32[64,512]{1,0:T(8,128)S(1)}, f32[64,512]{1,0:T(8,128)S(1)}, u32[]{:S(2)}, u32[]{:S(2)}) collective-permute-start(f32[64,512]{1,0:T(8,128)S(1)} %slice_bitcast_fusion), channel_id=1, source_target_pairs={{0,6},{1,7},{2,0},{3,1},{4,2},{5,3},{6,4},{7,5},{8,14},{9,15},{10,... | collective-permute-start | bytes 393224 | tf_op jit(solution)/shard_map/ppermute | solution.py:308
  19.3 13.5 %collective-permute-start.9 = (f32[64,512]{1,0:T(8,128)S(1)}, f32[64,512]{1,0:T(8,128)S(1)}, u32[]{:S(2)}, u32[]{:S(2)}) collective-permute-start(f32[64,512]{1,0:T(8,128)S(1)} %get-tuple-element.28.refs_0_), channel_id=1, source_target_pairs={{0,6},{1,7},{2,0},{3,1},{4,2},{5,3},{6,4},{7,5},{8,14},{9,15},{10,... | collective-permute-start | bytes 393224 | tf_op jit(solution)/shard_map/ppermute | solution.py:308
  19.4 13.4 %collective-permute-start.8 = (f32[64,512]{1,0:T(8,128)S(1)}, f32[64,512]{1,0:T(8,128)S(1)}, u32[]{:S(2)}, u32[]{:S(2)}) collective-permute-start(f32[64,512]{1,0:T(8,128)S(1)} %collective-permute-done.6.refs_1_), channel_id=1, source_target_pairs={{0,2},{1,3},{2,4},{3,5},{4,6},{5,7},{6,0},{7,1},{8,10},{9,11},{10,... | collective-permute-start | bytes 393224 | tf_op jit(solution)/shard_map/ppermute | solution.py:308
  20.8 12.1 %collective-permute-start.11 = (f32[64,512]{1,0:T(8,128)S(1)}, f32[64,512]{1,0:T(8,128)S(1)}, u32[]{:S(2)}, u32[]{:S(2)}) collective-permute-start(f32[64,512]{1,0:T(8,128)S(1)} %collective-permute-done.7.refs_2_), channel_id=1, source_target_pairs={{0,2},{1,3},{2,4},{3,5},{4,6},{5,7},{6,0},{7,1},{8,10},{9,11},{10,... | collective-permute-start | bytes 393224 | tf_op jit(solution)/shard_map/ppermute | solution.py:308
  20.9 12.0 %collective-permute-start.12 = (f32[64,512]{1,0:T(8,128)S(1)}, f32[64,512]{1,0:T(8,128)S(1)}, u32[]{:S(2)}, u32[]{:S(2)}) collective-permute-start(f32[64,512]{1,0:T(8,128)S(1)} %collective-permute-done.10.refs_5_), channel_id=1, source_target_pairs={{0,6},{1,7},{2,0},{3,1},{4,2},{5,3},{6,4},{7,5},{8,14},{9,15},{10,... | collective-permute-start | bytes 393224 | tf_op jit(solution)/shard_map/ppermute | solution.py:308
  29.9 5.5 %collective-permute-start.5 = (f32[3,64,512]{2,1,0:T(8,128)S(1)}, f32[3,64,512]{2,1,0:T(8,128)S(1)}, u32[]{:S(2)}, u32[]{:S(2)}) collective-permute-start(f32[3,64,512]{2,1,0:T(8,128)S(1)} %get-tuple-element.26), channel_id=1, source_target_pairs={{0,1},{1,0},{2,3},{3,2},{4,5},{5,4},{6,7},{7,6},{8,9},{9,8},{10,11... | collective-permute-start | bytes 1179656 | tf_op jit(solution)/shard_map/ppermute | solution.py:308
  32.9 2.6 %copy-start.2 = (f32[1,2,64,2,512]{4,3,2,1,0:T(2,128)S(1)}, f32[1,2,64,2,512]{4,3,2,1,0:T(2,128)}, u32[]{:S(2)}) copy-start(f32[1,2,64,2,512]{4,3,2,1,0:T(2,128)} %param.9) | copy-start | bytes 1572868
  32.9 2.6 %copy-start.4 = (f32[1,8,8]{2,1,0:T(8,128)S(1)}, f32[1,8,8]{2,1,0:T(8,128)}, u32[]{:S(2)}) copy-start(f32[1,8,8]{2,1,0:T(8,128)} %param.13) | copy-start | bytes 772
  35.3 1.8 %collective-permute-start.13 = (f32[3,64,512]{2,1,0:T(8,128)S(1)}, f32[3,64,512]{2,1,0:T(8,128)S(1)}, u32[]{:S(2)}, u32[]{:S(2)}) collective-permute-start(f32[3,64,512]{2,1,0:T(8,128)S(1)} %get-tuple-element.34), channel_id=1, source_target_pairs={{0,1},{1,0},{2,3},{3,2},{4,5},{5,4},{6,7},{7,6},{8,9},{9,8},{10,11... | collective-permute-start | bytes 1179656 | tf_op jit(solution)/shard_map/ppermute | solution.py:308
  39.4 18.7 %all-to-all-start = ((f32[32,8,128]{2,1,0:T(8,128)}), f32[32,8,128]{2,1,0:T(8,128)S(1)}, u32[]{:S(2)}, u32[]{:S(2)}) async-start(f32[32,8,128]{2,1,0:T(8,128)} %get-tuple-element.37), calls=%async_computation | async-start | bytes 262144 | tf_op jit(solution)/shard_map/all_to_all | solution.py:369
